TPU v7x, 256 devices: a whole 4x4x8 slice. The times are simulated.
256 devices in a mesh: branch: 32 (over z, y_lo, core), bus: 8 (over x, y_hi).
Axes of the slice: x: 4, y: 4 (y_hi: 2, y_lo: 2; y = y_hi * 2 + y_lo), z: 8, core: 2. Of those that a mesh axis runs over, the one named last changes fastest.
Arguments:
- injections: float32 [512, 60416], P('branch', 'bus'), may hold values from -0.0234375 to 0.0234375
- ptdf_mon: float32 [4096, 60416], P('branch', 'bus'), may hold values from -2.5 to 2.5
- ptdf_out: float32 [2048, 60416], P('branch', 'bus'), may hold values from -2.5 to 2.5
- outage_from: int32 [2048], replicated, may hold values from 0 to 60415
- outage_to: int32 [2048], replicated, may hold values from 0 to 60415
- hour_ids: int32 [512], P('bus'), may hold values from 0 to 8759
- ratings: float32 [4096, 4], P('branch'), may hold values from 0.5 to 2
Outputs:
- worst_loading: float32 [512, 4096], P('bus', 'branch')
All inputs are finite; a program needn't handle non-finite values.
Results may differ from a plain program's by a relative error of at most 0.00019.
Values sent between devices are 32-bit elements; how exact they have to be, the bound alone decides.
A program may use at most 128 MiB of HBM per device.

v0:
```python
import jax
import jax.numpy as jnp
from jax import lax
from jax.sharding import PartitionSpec as P


def screen(base_mon, outage_base, lodf_t, block_size):
    outage_count = lodf_t.shape[0]

    def advance(index, worst_load):
        first = index * block_size
        lodf_block = lax.dynamic_slice_in_dim(lodf_t, first, block_size, 0)
        flow_block = lax.dynamic_slice_in_dim(outage_base, first, block_size, 1)
        after_outage = base_mon[:, None, :] + flow_block[:, :, None] * lodf_block[None, :, :]
        return jnp.maximum(worst_load, jnp.max(jnp.abs(after_outage), axis=1))

    return lax.fori_loop(0, outage_count // block_size, advance, jnp.abs(base_mon))


def on_device(injections, ptdf_mon, ptdf_out, outage_from, outage_to, hour_ids, ratings):
    highest = lax.Precision.HIGHEST
    mon_rows = ptdf_mon.shape[0]
    out_rows = ptdf_out.shape[0]
    bus_width = ptdf_mon.shape[1]
    bus_count = lax.axis_size("bus")
    bus_index = lax.axis_index("bus")
    contract = (((1,), (1,)), ((), ()))
    piece = lax.all_gather(injections, "branch", axis=0, tiled=True)
    monitored = lax.dot_general(
        piece, ptdf_mon, contract, precision=highest, preferred_element_type=jnp.float32
    )
    outaged = lax.dot_general(
        piece, ptdf_out, contract, precision=highest, preferred_element_type=jnp.float32
    )
    partial_flows = jnp.concatenate([monitored, outaged], axis=1)
    hours_dev = partial_flows.shape[0] // bus_count
    summed_flows = lax.psum(partial_flows, "bus")
    base_flows = lax.dynamic_slice_in_dim(summed_flows, bus_index * hours_dev, hours_dev, 0)
    offset = bus_index * bus_width

    def localize(bus_ids):
        shifted = bus_ids - offset
        inside = jnp.logical_and(shifted >= 0, shifted < bus_width).astype(jnp.float32)
        return (jnp.clip(shifted, 0, bus_width - 1), inside)

    from_index, from_inside = localize(outage_from)
    to_index, to_inside = localize(outage_to)

    def columns(matrix):
        return (
            jnp.take(matrix, from_index, axis=1) * from_inside[None, :]
            - jnp.take(matrix, to_index, axis=1) * to_inside[None, :]
        )

    first_outage = lax.axis_index("branch") * out_rows
    sens_mon, sens_out = lax.psum((columns(ptdf_mon), columns(ptdf_out)), "bus")
    self_sens = jnp.diagonal(lax.dynamic_slice_in_dim(sens_out, first_outage, out_rows, 1))
    base_mon = base_flows[:, :mon_rows]
    base_out = base_flows[:, mon_rows:]
    outage_base, outage_self = (
        lax.all_gather(base_out, "branch", axis=1, tiled=True),
        lax.all_gather(self_sens, "branch", axis=0, tiled=True),
    )
    divisor = jnp.maximum(1.0 - outage_self, 0.25)
    lodf_t = (sens_mon / divisor[None, :]).T
    worst_load = screen(base_mon, outage_base, lodf_t, min(256, lodf_t.shape[0]))
    season = hour_ids * 4 // 8760
    onehot = (season[:, None] == jnp.arange(ratings.shape[1], dtype=jnp.int32)[None, :]).astype(
        jnp.float32
    )
    hour_rating = jnp.dot(onehot, ratings.T, precision=highest, preferred_element_type=jnp.float32)
    return worst_load / hour_rating


def solution(mesh):
    placed = (
        P("branch", "bus"),
        P("branch", "bus"),
        P("branch", "bus"),
        P(),
        P(),
        P("bus"),
        P("branch", None),
    )
    return jax.shard_map(
        on_device, mesh=mesh, in_specs=placed, out_specs=P("bus", "branch"), check_vma=False
    )
```

profile of v0, /device:TPU:6, one launch (start us, length us, event | category | flops | bytes accessed | tf_op | source)
XLA Modules:
  0.0 396.1 jit_solution(17618373268766414951)
XLA Ops:
  7.3 5.4 %copy.22 = f32[128,7552]{0,1:T(8,128)} copy(f32[128,7552]{1,0:T(8,128)} %param.14) | data formatting | bytes 7733248 | tf_op args[1]
  12.7 7.6 %gather_fusion.2 = f32[2048,128]{1,0:T(8,128)S(1)} fusion(f32[128,7552]{0,1:T(8,128)} %copy.22, s32[2048]{0:T(1024)S(1)} %get-tuple-element.139), kind=kCustom, calls=%fused_computation.2.clone | custom fusion | bytes 2105344 | tf_op jit(solution)/shard_map/jit(_take)/gather | solution.py:52
  20.3 9.8 %gather_fusion.1 = f32[2048,128]{1,0:T(8,128)} fusion(f32[128,7552]{0,1:T(8,128)} %copy.22, s32[2048]{0:T(1024)S(1)} %get-tuple-element.138), kind=kCustom, calls=%fused_computation.clone | custom fusion | bytes 2105344 | tf_op jit(solution)/shard_map/jit(_take)/gather | solution.py:51
  30.1 2.7 copy.24
  32.9 9.8 %gather_fusion.4 = f32[2048,64]{1,0:T(8,128)} fusion(f32[64,7552]{0,1:T(8,128)} %copy.24, s32[2048]{0:T(1024)S(1)} %get-tuple-element.139), kind=kCustom, calls=%fused_computation.3.clone | custom fusion | bytes 1056768 | tf_op jit(solution)/shard_map/jit(_take)/gather | solution.py:52
  42.7 9.8 %gather_fusion.3 = f32[2048,64]{1,0:T(8,128)} fusion(f32[64,7552]{0,1:T(8,128)} %copy.24, s32[2048]{0:T(1024)S(1)} %get-tuple-element.138), kind=kCustom, calls=%fused_computation.1.clone | custom fusion | bytes 1056768 | tf_op jit(solution)/shard_map/jit(_take)/gather | solution.py:51
  52.5 4.4 %fusion.1 = f32[128,2048]{0,1:T(8,128)} fusion(f32[2048,128]{1,0:T(8,128)S(1)} %gather_fusion.2, f32[2048,128]{1,0:T(8,128)} %gather_fusion.1, f32[2048]{0:T(1024)S(1)} %get-tuple-element.135, f32[2048]{0:T(1024)S(1)} %get-tuple-element.136, pred[2048]{0:T(1024)(128)(4,1)S(1)} %get-tuple-element.134, pred[2048]{0:T(1024)(128)(4,1)S(1)} %get-tuple-element.137), kind=kLoop, calls=%fused_computation.13 | loop fusion | flops 1310720 | bytes 3166208 | tf_op jit(solution)/shard_map/sub | solution.py:51
  56.9 2.9 fusion
  59.8 45.4 %all-gather.2.cloned.1.call-done = f32[512,7552]{1,0:T(8,128)} async-done(((f32[16,7552]{1,0:T(8,128)}), f32[512,7552]{1,0:T(8,128)}) %all-gather.2.cloned.1.call-update) | async-done | bytes 15466512 | tf_op jit(solution)/shard_map/all_gather | solution.py:28
  105.2 19.0 %fusion.7 = f32[512,64]{0,1:T(8,128)S(1)} fusion(f32[512,7552]{1,0:T(8,128)} %all-gather.2.cloned.1.call-done, f32[64,7552]{1,0:T(8,128)S(1)} %copy-done.3), kind=kOutput, calls=%fused_computation.34 | convolution fusion | flops 2969567232 | bytes 17530880 | tf_op jit(solution)/shard_map/dot_general | solution.py:32
  124.3 16.4 %fusion.6 = f32[512,128]{0,1:T(8,128)S(1)} fusion(f32[512,7552]{1,0:T(8,128)S(1)} %copy-done.1, f32[128,7552]{1,0:T(8,128)S(1)} %copy-done.2), kind=kOutput, calls=%fused_computation.33 | convolution fusion | flops 5939134464 | bytes 19595264 | tf_op jit(solution)/shard_map/dot_general | solution.py:29
  142.9 128.5 %all-reduce.4.cloned.1.call-done = (f32[512,192]{0,1:T(8,128)}, f32[128,2048]{0,1:T(8,128)}, f32[64,2048]{0,1:T(8,128)}) async-done(((f32[512,192]{0,1:T(8,128)}, f32[128,2048]{0,1:T(8,128)}, f32[64,2048]{0,1:T(8,128)}), (f32[512,192]{0,1:T(8,128)}, f32[128,2048]{0,1:T(8,128)}, f32[64,2048]{0,1:T(8,128)})) %all-reduce.4.cloned.1.call-update) | async-done | bytes 1966096 | tf_op jit(solution)/shard_map/psum | solution.py:37
  271.4 1.0 fusion.5
  273.4 36.4 %all_gather.10 = f32[64,2048]{0,1:T(8,128)S(1)} all-gather(f32[64,64]{0,1:T(8,128)S(1)} %dynamic-slice.2), channel_id=1, replica_groups=mesh['branch'=32,'bus'=8] {'branch'}, dimensions={1}, use_global_device_ids=true | all-gather | bytes 540672 | tf_op jit(solution)/shard_map/all_gather | solution.py:61
  312.0 54.3 %all-reduce = f32[2048]{0:T(1024)S(1)} all-reduce(f32[2048]{0:T(1024)S(1)} %dynamic-update-slice), channel_id=1, replica_groups=mesh['branch'=32,'bus'=8] {'branch'}, use_global_device_ids=true, to_apply=%add | all-reduce | flops 2048 | bytes 16384
  366.7 21.7 %while.13 = (s32[]{:T(128)}, f32[64,128]{1,0:T(8,128)S(1)}, f32[64,128]{1,0:T(8,128)S(1)}, f32[64,2048]{1,0:T(8,128)S(1)}, f32[2048,128]{1,0:T(8,128)S(1)}, /*index=5*/s32[]{:T(128)}, s32[]{:T(128)}, s32[]{:T(128)}, s32[]{:T(128)}) while((s32[]{:T(128)}, f32[64,128]{1,0:T(8,128)S(1)}, f32[64,128]{1,0:T(8,128)S(1)}, f32[64,2048]{1,0:T(8,128)S(1)}, ...), condition=%wide.region_5.8_spmd, body=%wide.region_3.7_spmd.sunk | while | flops 8388614 | bytes 753819 | solution.py:17
  366.8 2.6 abs_reduce_fusion.2
  369.5 2.6 abs_reduce_fusion.2
  372.2 2.6 abs_reduce_fusion.2
  374.9 2.6 abs_reduce_fusion.2
  377.6 2.6 abs_reduce_fusion.2
  380.3 2.6 abs_reduce_fusion.2
  383.1 2.6 abs_reduce_fusion.2
  385.8 2.6 abs_reduce_fusion.2
  (67 shorter events, 6.9 us)
Async XLA Ops:
  6.5 381.9 %copy-start = (f32[128,4]{0,1:T(4,128)S(1)}, f32[128,4]{0,1:T(4,128)}, u32[]{:S(2)}) copy-start(f32[128,4]{0,1:T(4,128)} %param.19) | copy-start | bytes 6148
  6.5 98.7 %all-gather.2.cloned.1.call-start = ((), (), s32[]{:S(2)}) async-start(), calls=%async_computation | async-start | bytes 15949824 | tf_op jit(solution)/shard_map/all_gather | solution.py:28
  7.3 264.1 %all-reduce.4.cloned.1.call-start = ((), (), s32[]{:S(2)}) async-start(), calls=%async_computation.1 | async-start | bytes 4980736 | tf_op jit(solution)/shard_map/psum | solution.py:37
  7.3 5.4 %copy-start.7 = (s32[2048]{0:T(1024)S(1)}, s32[2048]{0:T(1024)}, u32[]{:S(2)}) copy-start(s32[2048]{0:T(1024)} %param.16) | copy-start | bytes 24580
  7.3 5.4 %copy-start.8 = (s32[2048]{0:T(1024)S(1)}, s32[2048]{0:T(1024)}, u32[]{:S(2)}) copy-start(s32[2048]{0:T(1024)} %param.17) | copy-start | bytes 24580
  20.3 9.9 %copy-start.3 = (f32[64,7552]{1,0:T(8,128)S(1)}, f32[64,7552]{1,0:T(8,128)}, u32[]{:S(2)}) copy-start(f32[64,7552]{1,0:T(8,128)} %param.15) | copy-start | bytes 5799940
  52.4 4.5 %copy-start.4 = (f32[2048,64]{1,0:T(8,128)S(1)}, f32[2048,64]{1,0:T(8,128)}, u32[]{:S(2)}) copy-start(f32[2048,64]{1,0:T(8,128)} %gather_fusion.4) | copy-start | bytes 1572868
  52.5 4.5 %copy-start.5 = (f32[2048,64]{1,0:T(8,128)S(1)}, f32[2048,64]{1,0:T(8,128)}, u32[]{:S(2)}) copy-start(f32[2048,64]{1,0:T(8,128)} %gather_fusion.3) | copy-start | bytes 1572868
  105.2 19.0 %copy-start.1 = (f32[512,7552]{1,0:T(8,128)S(1)}, f32[512,7552]{1,0:T(8,128)}, u32[]{:S(2)}) copy-start(f32[512,7552]{1,0:T(8,128)} %all-gather.2.cloned.1.call-done) | copy-start | bytes 46399492
  105.2 19.0 %copy-start.2 = (f32[128,7552]{1,0:T(8,128)S(1)}, f32[128,7552]{1,0:T(8,128)}, u32[]{:S(2)}) copy-start(f32[128,7552]{1,0:T(8,128)} %param.14) | copy-start | bytes 11599876
  124.2 17.2 %copy-start.10 = (u32[256]{0:T(256)S(1)}, u32[256]{0:T(256)}, u32[]{:S(2)}) copy-start(u32[256]{0:T(256)} %constant.114) | copy-start | bytes 3076
  124.3 18.6 %copy-start.9 = (s32[64]{0:T(128)S(1)}, s32[64]{0:T(128)}, u32[]{:S(2)}) copy-start(s32[64]{0:T(128)} %param.18) | copy-start | bytes 772
  271.4 94.9 %copy-start.6 = (f32[128,2048]{0,1:T(8,128)S(1)}, f32[128,2048]{0,1:T(8,128)}, u32[]{:S(2)}) copy-start(f32[128,2048]{0,1:T(8,128)} %get-tuple-element.128) | copy-start | bytes 3145732
Sparse Core Ops, SparseCore 0:
  9.2 95.9 all-gather.1
  141.6 129.7 all-reduce.3
where the time goes:
time: 397 us; the launch traced here: 396 us
  waiting for transfers between devices  175 us (44%)
  blocking collectives  90.7 us (23%)
  local copies, waits for them, and re-layouts  49.2 us (12%)
  matrix products  36.2 us (9%)
  other arithmetic  30.6 us (8%)
  between operations  14.3 us (4%)
    psum x1, waiting for transfers between devices, on_device(): summed_flows = lax.psum(partial_flows, 'bus')  129 us
    unnamed x1, blocking collectives  54.3 us
    all_gather x1, waiting for transfers between devices, on_device(): piece = lax.all_gather(injections, 'branch', axis=0, tiled=True)  45.4 us
    all_gather x1, blocking collectives, on_device(): lax.all_gather(base_out, 'branch', axis=1, tiled=True)  36.4 us
    reduce_max x8, other arithmetic, advance(): return jnp.maximum(worst_load, jnp.max(jnp.abs(after_outage), axis=1))  21 us
    gather x2, local copies, waits for them, and re-layouts, columns(): jnp.take(matrix, from_index, axis=1) * from_inside[None, :]  19.6 us
    dot_general x1, matrix products, on_device(): lax.dot_general(piece, ptdf_out, contract, precision=highest, preferred_e...  19 us
    gather x2, local copies, waits for them, and re-layouts, columns(): jnp.take(matrix, to_index, axis=1) * to_inside[None, :]  17.3 us
  transfers between devices with their start and end apart: 2, of which 2 were waited for; matrix products, arithmetic and copies ran while one was open for 13% of the time, Pallas kernels for 0%

commit v1 on v0

--- a/solution.py
+++ b/solution.py
@@ -25,7 +25,10 @@
     bus_count = lax.axis_size("bus")
     bus_index = lax.axis_index("bus")
     contract = (((1,), (1,)), ((), ()))
-    piece = lax.all_gather(injections, "branch", axis=0, tiled=True)
+    size = lax.axis_size("branch")
+    blocks = jnp.stack([injections for _ in range(size)])
+    blocks = lax.all_to_all(blocks, "branch", split_axis=0, concat_axis=0)
+    piece = jnp.concatenate(blocks, axis=0)
     monitored = lax.dot_general(
         piece, ptdf_mon, contract, precision=highest, preferred_element_type=jnp.float32
     )

time: 397 us -> 652 us (1.64)
  waiting for transfers between devices: 175 us -> 410 us
  starting transfers between devices: 0.04 us -> 10.2 us
  local copies, waits for them, and re-layouts: 49.2 us -> 56.3 us
    all_to_all x0 -> x1, waiting for transfers between devices: none -> 284 us  [on_device(): blocks = lax.all_to_all(blocks, 'branch', split_axis=0, concat_axis=0)]
    all_gather x1 -> x0, waiting for transfers between devices: 45.4 us -> none  [on_device(): piece = lax.all_gather(injections, 'branch', axis=0, tiled=True)]
    all_to_all x0 -> x1, starting transfers between devices: none -> 10.1 us  [on_device(): blocks = lax.all_to_all(blocks, 'branch', split_axis=0, concat_axis=0)]
    another operation x0 -> x1, local copies, waits for them, and re-layouts: none -> 7.47 us  [on_device(): blocks = jnp.stack([injections for _ in range(size)])]
  transfers between devices with their start and end apart: 2 -> 2, of which waited for: 2 -> 2; matrix products, arithmetic and copies ran while one was open for 13% -> 8% of each run, Pallas kernels for 0% -> 0%
where the time goes in v1:
time: 652 us; the launch traced here: 651 us
  waiting for transfers between devices  410 us (63%)
  blocking collectives  90.7 us (14%)
  local copies, waits for them, and re-layouts  56.3 us (9%)
  matrix products  36.2 us (6%)
  other arithmetic  33.2 us (5%)
  between operations  14.3 us (2%)
  starting transfers between devices  10.2 us (2%)
    all_to_all x1, waiting for transfers between devices, on_device(): blocks = lax.all_to_all(blocks, 'branch', split_axis=0, concat_axis=0)  284 us
    psum x1, waiting for transfers between devices, on_device(): summed_flows = lax.psum(partial_flows, 'bus')  125 us
    unnamed x1, blocking collectives  54.3 us
    all_gather x1, blocking collectives, on_device(): lax.all_gather(base_out, 'branch', axis=1, tiled=True)  36.4 us
    reduce_max x8, other arithmetic, advance(): return jnp.maximum(worst_load, jnp.max(jnp.abs(after_outage), axis=1))  21 us
    gather x2, local copies, waits for them, and re-layouts, columns(): jnp.take(matrix, from_index, axis=1) * from_inside[None, :]  19.3 us
    dot_general x1, matrix products, on_device(): lax.dot_general(piece, ptdf_mon, contract, precision=highest, preferred_e...  18 us
    gather x2, local copies, waits for them, and re-layouts, columns(): jnp.take(matrix, to_index, axis=1) * to_inside[None, :]  17.4 us
  transfers between devices with their start and end apart: 2, of which 2 were waited for; matrix products, arithmetic and copies ran while one was open for 8% of the time, Pallas kernels for 0%

profile of v1, /device:TPU:6, one launch (start us, length us, event | category | flops | bytes accessed | tf_op | source)
XLA Modules:
  0.0 650.9 jit_solution(11225687527241459590)
XLA Ops:
  6.5 7.5 %stack.2 = f32[32,16,7552]{2,1,0:T(8,128)} broadcast(f32[16,7552]{1,0:T(8,128)} %param.13), dimensions={1,2} | broadcast | bytes 15949824 | tf_op jit(solution)/shard_map/stack | solution.py:29
  14.0 10.1 %all-to-all-start = ((f32[32,16,7552]{2,1,0:T(8,128)}), f32[32,16,7552]{2,1,0:T(8,128)}, u32[]{:S(2)}, u32[]{:S(2)}) async-start(f32[32,16,7552]{2,1,0:T(8,128)} %stack.2), calls=%async_computation | async-start | bytes 30932992 | tf_op jit(solution)/shard_map/all_to_all | solution.py:30
  24.2 5.4 copy.22
  29.6 7.7 %gather_fusion.2 = f32[2048,128]{1,0:T(8,128)S(1)} fusion(f32[128,7552]{0,1:T(8,128)} %copy.22, s32[2048]{0:T(1024)S(1)} %get-tuple-element.139), kind=kCustom, calls=%fused_computation.2.clone | custom fusion | bytes 2105344 | tf_op jit(solution)/shard_map/jit(_take)/gather | solution.py:55
  37.3 9.7 %gather_fusion.1 = f32[2048,128]{1,0:T(8,128)} fusion(f32[128,7552]{0,1:T(8,128)} %copy.22, s32[2048]{0:T(1024)S(1)} %get-tuple-element.138), kind=kCustom, calls=%fused_computation.clone | custom fusion | bytes 2105344 | tf_op jit(solution)/shard_map/jit(_take)/gather | solution.py:54
  47.0 2.6 copy.24
  49.6 9.7 %gather_fusion.4 = f32[2048,64]{1,0:T(8,128)} fusion(f32[64,7552]{0,1:T(8,128)} %copy.24, s32[2048]{0:T(1024)S(1)} %get-tuple-element.139), kind=kCustom, calls=%fused_computation.3.clone | custom fusion | bytes 1056768 | tf_op jit(solution)/shard_map/jit(_take)/gather | solution.py:55
  59.3 9.7 %gather_fusion.3 = f32[2048,64]{1,0:T(8,128)} fusion(f32[64,7552]{0,1:T(8,128)} %copy.24, s32[2048]{0:T(1024)S(1)} %get-tuple-element.138), kind=kCustom, calls=%fused_computation.1.clone | custom fusion | bytes 1056768 | tf_op jit(solution)/shard_map/jit(_take)/gather | solution.py:54
  69.0 4.3 fusion.1
  73.3 4.5 fusion
  77.7 284.4 %all-to-all-done = f32[32,16,7552]{2,1,0:T(8,128)} async-done(((f32[32,16,7552]{2,1,0:T(8,128)}), f32[32,16,7552]{2,1,0:T(8,128)}, u32[]{:S(2)}, u32[]{:S(2)}) %all-to-all-start) | async-done | bytes 15466528 | tf_op jit(solution)/shard_map/all_to_all | solution.py:30
  362.2 17.3 %fusion.7 = f32[512,64]{0,1:T(8,128)S(1)} fusion(f32[512,7552]{1,0:T(8,128)} %bitcast, f32[64,7552]{1,0:T(8,128)S(1)} %copy-done.2), kind=kOutput, calls=%fused_computation.34 | convolution fusion | flops 2969567232 | bytes 17530880 | tf_op jit(solution)/shard_map/dot_general | solution.py:35
  379.5 18.0 %fusion.6 = f32[512,128]{0,1:T(8,128)S(1)} fusion(f32[512,7552]{1,0:T(8,128)} %bitcast, f32[128,7552]{1,0:T(8,128)S(1)} %copy-done.1), kind=kOutput, calls=%fused_computation.33 | convolution fusion | flops 5939134464 | bytes 19595264 | tf_op jit(solution)/shard_map/dot_general | solution.py:32
  399.8 125.3 %all-reduce.4.cloned.1.call-done = (f32[512,192]{0,1:T(8,128)}, f32[128,2048]{0,1:T(8,128)}, f32[64,2048]{0,1:T(8,128)}) async-done(((f32[512,192]{0,1:T(8,128)}, f32[128,2048]{0,1:T(8,128)}, f32[64,2048]{0,1:T(8,128)}), (f32[512,192]{0,1:T(8,128)}, f32[128,2048]{0,1:T(8,128)}, f32[64,2048]{0,1:T(8,128)})) %all-reduce.4.cloned.1.call-update) | async-done | bytes 1966096 | tf_op jit(solution)/shard_map/psum | solution.py:40
  527.0 36.4 %all_gather.6 = f32[64,2048]{0,1:T(8,128)S(1)} all-gather(f32[64,64]{0,1:T(8,128)S(1)} %dynamic-slice.2), channel_id=1, replica_groups=mesh['branch'=32,'bus'=8] {'branch'}, dimensions={1}, use_global_device_ids=true | all-gather | bytes 540672 | tf_op jit(solution)/shard_map/all_gather | solution.py:64
  565.6 54.3 %all-reduce = f32[2048]{0:T(1024)S(1)} all-reduce(f32[2048]{0:T(1024)S(1)} %dynamic-update-slice), channel_id=1, replica_groups=mesh['branch'=32,'bus'=8] {'branch'}, use_global_device_ids=true, to_apply=%add | all-reduce | flops 2048 | bytes 16384
  621.5 21.7 %while.13 = (s32[]{:T(128)}, f32[64,128]{1,0:T(8,128)S(1)}, f32[64,128]{1,0:T(8,128)S(1)}, f32[64,2048]{1,0:T(8,128)S(1)}, f32[2048,128]{1,0:T(8,128)S(1)}, /*index=5*/s32[]{:T(128)}, s32[]{:T(128)}, s32[]{:T(128)}, s32[]{:T(128)}) while((s32[]{:T(128)}, f32[64,128]{1,0:T(8,128)S(1)}, f32[64,128]{1,0:T(8,128)S(1)}, f32[64,2048]{1,0:T(8,128)S(1)}, ...), condition=%wide.region_5.8_spmd, body=%wide.region_3.7_spmd.sunk | while | flops 8388614 | bytes 753819 | solution.py:17
  621.6 2.6 abs_reduce_fusion.2
  624.3 2.6 abs_reduce_fusion.2
  627.0 2.6 abs_reduce_fusion.2
  629.7 2.6 abs_reduce_fusion.2
  632.4 2.6 abs_reduce_fusion.2
  635.2 2.6 abs_reduce_fusion.2
  637.9 2.6 abs_reduce_fusion.2
  (59 shorter events, 11.0 us)
Async XLA Ops:
  6.5 636.7 %copy-start = (f32[128,4]{0,1:T(4,128)S(1)}, f32[128,4]{0,1:T(4,128)}, u32[]{:S(2)}) copy-start(f32[128,4]{0,1:T(4,128)} %param.19) | copy-start | bytes 6148
  14.0 15.6 %copy-start.3 = (s32[2048]{0:T(1024)S(1)}, s32[2048]{0:T(1024)}, u32[]{:S(2)}) copy-start(s32[2048]{0:T(1024)} %param.16) | copy-start | bytes 24580
  14.0 15.6 %copy-start.4 = (s32[2048]{0:T(1024)S(1)}, s32[2048]{0:T(1024)}, u32[]{:S(2)}) copy-start(s32[2048]{0:T(1024)} %param.17) | copy-start | bytes 24580
  14.0 348.2 %all-to-all-start = ((f32[32,16,7552]{2,1,0:T(8,128)}), f32[32,16,7552]{2,1,0:T(8,128)}, u32[]{:S(2)}, u32[]{:S(2)}) async-start(f32[32,16,7552]{2,1,0:T(8,128)} %stack.2), calls=%async_computation | async-start | bytes 30932992 | tf_op jit(solution)/shard_map/all_to_all | solution.py:30
  24.1 501.0 %all-reduce.4.cloned.1.call-start = ((), (), s32[]{:S(2)}) async-start(), calls=%async_computation.1 | async-start | bytes 4980736 | tf_op jit(solution)/shard_map/psum | solution.py:40
  29.6 17.4 %copy-start.2 = (f32[64,7552]{1,0:T(8,128)S(1)}, f32[64,7552]{1,0:T(8,128)}, u32[]{:S(2)}) copy-start(f32[64,7552]{1,0:T(8,128)} %param.15) | copy-start | bytes 5799940
  362.2 17.3 %copy-start.1 = (f32[128,7552]{1,0:T(8,128)S(1)}, f32[128,7552]{1,0:T(8,128)}, u32[]{:S(2)}) copy-start(f32[128,7552]{1,0:T(8,128)} %param.14) | copy-start | bytes 11599876
  379.5 18.9 %copy-start.6 = (u32[256]{0:T(256)S(1)}, u32[256]{0:T(256)}, u32[]{:S(2)}) copy-start(u32[256]{0:T(256)} %constant.114) | copy-start | bytes 3076
  379.5 20.2 %copy-start.5 = (s32[64]{0:T(128)S(1)}, s32[64]{0:T(128)}, u32[]{:S(2)}) copy-start(s32[64]{0:T(128)} %param.18) | copy-start | bytes 772
Sparse Core Ops, SparseCore 0:
  398.5 126.5 all-reduce.3
